TPU v7x, 32 devices: a whole 2x2x4 slice. The times are simulated.
32 devices in a mesh: seq: 16 (over z, x, core), head: 2 (over y).
Axes of the slice: x: 2, y: 2, z: 4, core: 2. Of those that a mesh axis runs over, the one named last changes fastest.
Arguments:
- alignment_rows: bfloat16 [128, 1024, 256], P('seq'), may hold values from -16 to 16
- upstream_derivative_tensor: bfloat16 [128, 1024, 256], P(None, 'seq'), may hold values from -12 to 12
- saved_pair_bias: bfloat16 [8, 1024, 1024], P('head', 'seq'), may hold values from -360 to 360
- pairwise_features: bfloat16 [1024, 1024, 128], P('seq', 'head'), may hold values from -16 to 16
- sequence_layernorm_scaling: float32 [256], replicated, may hold values from 0.5 to 2
- sequence_layernorm_centre: float32 [256], replicated, may hold values from -1 to 1
- asking_projection_matrix: bfloat16 [256, 256], replicated, may hold values from -0.375 to 0.375
- matching_projection_matrix: bfloat16 [256, 256], replicated, may hold values from -0.375 to 0.375
- content_projection_matrix: bfloat16 [256, 256], replicated, may hold values from -0.375 to 0.375
- sigmoid_projection_matrix: bfloat16 [256, 256], replicated, may hold values from -0.375 to 0.375
- gate_offset_bias: float32 [256], replicated, may hold values from -2 to 2
- final_projection_matrix: bfloat16 [256, 256], replicated, may hold values from -0.375 to 0.375
- pairwise_norm_gain: float32 [128], replicated, may hold values from 0.5 to 2
- pairwise_weight: bfloat16 [128, 8], replicated, may hold values from -0.5 to 0.5
Outputs:
- alignment_input_gradient: bfloat16 [128, 1024, 256], P('seq', 'head')
- pairwise_gradient: bfloat16 [1024, 1024, 128], P('seq', 'head')
All inputs are finite; a program needn't handle non-finite values.
Results may differ from a plain program's by a relative error of at most 0.012.
The roundings to bfloat16 on the way count: a program that leaves them out, or rounds other values in their place, can miss the bound.
Values may be sent and summed in bfloat16 or wider, within the bound.
A program may use at most 320 MiB of HBM per device.

v0:
```python
import jax
import jax.numpy as jnp
from jax import lax
from jax.sharding import PartitionSpec as P

SUBSPACE_WIDTH = 32


epsilon = 1e-05


def layer_statistics(values):
    average = jnp.mean(values, axis=-1, keepdims=True)
    centred = values - average
    inverse_deviation = lax.rsqrt(jnp.mean(centred * centred, axis=-1, keepdims=True) + epsilon)
    return (centred * inverse_deviation, inverse_deviation)


def layer_reverse_step(upstream, standardized_values, inverse_deviation):
    first_mean = jnp.mean(upstream, axis=-1, keepdims=True)
    second_mean = jnp.mean(upstream * standardized_values, axis=-1, keepdims=True)
    return inverse_deviation * (upstream - first_mean - standardized_values * second_mean)


def per_device(
    alignment_rows,
    upstream_derivative_tensor,
    saved_pair_bias,
    pairwise_features,
    sequence_layernorm_scaling,
    sequence_layernorm_centre,
    asking_projection_matrix,
    matching_projection_matrix,
    content_projection_matrix,
    sigmoid_projection_matrix,
    gate_offset_bias,
    final_projection_matrix,
    pairwise_norm_gain,
    pairwise_weight,
):
    local_heads = saved_pair_bias.shape[0]
    all_heads = pairwise_weight.shape[1]
    resident_rows, residue_total, channel_count = alignment_rows.shape
    head_width = local_heads * SUBSPACE_WIDTH
    first_head = lax.axis_index("head") * local_heads
    first_col = first_head * SUBSPACE_WIDTH
    score_scale = SUBSPACE_WIDTH ** (-0.5)
    bias_full = lax.all_gather(saved_pair_bias, "seq", axis=1, tiled=True)
    standardized_values, inverse_deviation = layer_statistics(alignment_rows.astype(jnp.float32))
    normalized_rows = (
        standardized_values * sequence_layernorm_scaling + sequence_layernorm_centre
    ).astype(jnp.bfloat16)

    def project(coefficient_matrix):
        columns = lax.dynamic_slice_in_dim(coefficient_matrix, first_col, head_width, 1)
        return jnp.dot(normalized_rows, columns, preferred_element_type=jnp.float32)

    head_shape = (resident_rows, residue_total, local_heads, SUBSPACE_WIDTH)
    query = (
        (score_scale * project(asking_projection_matrix)).astype(jnp.bfloat16).reshape(head_shape)
    )
    keys_all = project(matching_projection_matrix).astype(jnp.bfloat16).reshape(head_shape)
    vals_all = project(content_projection_matrix).astype(jnp.bfloat16).reshape(head_shape)
    gate_shift = lax.dynamic_slice_in_dim(gate_offset_bias, first_col, head_width, 0)
    gate = jax.nn.sigmoid(project(sigmoid_projection_matrix) + gate_shift).reshape(head_shape)
    out_rows = lax.dynamic_slice_in_dim(final_projection_matrix, first_col, head_width, 0)
    row_grads = lax.all_to_all(
        upstream_derivative_tensor, "seq", split_axis=0, concat_axis=1, tiled=True
    )
    gated_grad = jnp.einsum(
        "src,wc->srw", row_grads, out_rows, preferred_element_type=jnp.float32
    ).astype(jnp.bfloat16)
    gated_grad = gated_grad.reshape(head_shape)
    bias_float = bias_full.astype(jnp.float32)

    def row_reverse_step(pair_bias_gradient, layer_inputs):
        query_row, keys_row, vals_row, gate_row, row_gradient = layer_inputs
        logits = (
            jnp.einsum("ihd,jhd->hij", query_row, keys_row, preferred_element_type=jnp.float32)
            + bias_float
        )
        probs = jax.nn.softmax(logits, axis=-1)
        probs_low = probs.astype(jnp.bfloat16)
        attended = jnp.einsum(
            "hij,jhd->ihd", probs_low, vals_row, preferred_element_type=jnp.float32
        )
        grad_float = row_gradient.astype(jnp.float32)
        attended_grad = (grad_float * gate_row).astype(jnp.bfloat16)
        gate_grad = (grad_float * attended * gate_row * (1.0 - gate_row)).astype(jnp.bfloat16)
        prob_grad = jnp.einsum(
            "ihd,jhd->hij", attended_grad, vals_row, preferred_element_type=jnp.float32
        )
        inner_sum = jnp.sum(probs * prob_grad, axis=-1, keepdims=True)
        score_grad = probs * (prob_grad - inner_sum)
        score_low = score_grad.astype(jnp.bfloat16)
        query_grad = (
            score_scale
            * jnp.einsum("hij,jhd->ihd", score_low, keys_row, preferred_element_type=jnp.float32)
        ).astype(jnp.bfloat16)
        key_grad = jnp.einsum(
            "hij,ihd->jhd", score_low, query_row, preferred_element_type=jnp.float32
        ).astype(jnp.bfloat16)
        value_grad = jnp.einsum(
            "hij,ihd->jhd", probs_low, attended_grad, preferred_element_type=jnp.float32
        ).astype(jnp.bfloat16)
        grads = jnp.concatenate([query_grad, key_grad, value_grad, gate_grad], axis=-1)
        return (pair_bias_gradient + score_grad, grads)

    pair_bias_gradient, head_grad_rows = lax.scan(
        row_reverse_step,
        jnp.zeros((local_heads, residue_total, residue_total), jnp.float32),
        (query, keys_all, vals_all, gate, gated_grad),
    )
    piled_arrays = jnp.stack(
        [
            coefficient_matrix.reshape(channel_count, all_heads, SUBSPACE_WIDTH)
            for coefficient_matrix in (
                asking_projection_matrix,
                matching_projection_matrix,
                content_projection_matrix,
                sigmoid_projection_matrix,
            )
        ],
        axis=2,
    )
    piled_arrays = piled_arrays.reshape(channel_count, all_heads, 4 * SUBSPACE_WIDTH)
    local_weight = lax.dynamic_slice_in_dim(piled_arrays, first_head, local_heads, 1)
    partial_term = jnp.einsum(
        "srhf,chf->src", head_grad_rows, local_weight, preferred_element_type=jnp.float32
    )
    normalized_gradient = lax.psum_scatter(
        partial_term.astype(jnp.bfloat16), "head", scatter_dimension=1, tiled=True
    ).astype(jnp.float32)
    block_len = residue_total // lax.axis_size("head")
    block_start = lax.axis_index("head") * block_len
    normalized_block = lax.dynamic_slice_in_dim(standardized_values, block_start, block_len, 1)
    inverse_spread_block = lax.dynamic_slice_in_dim(inverse_deviation, block_start, block_len, 1)
    alignment_input_gradient = layer_reverse_step(
        normalized_gradient * sequence_layernorm_scaling, normalized_block, inverse_spread_block
    ).astype(jnp.bfloat16)
    summed_rows = lax.psum_scatter(pair_bias_gradient, "seq", scatter_dimension=1, tiled=True)
    bias_tile = lax.all_to_all(
        summed_rows.astype(jnp.bfloat16), "head", split_axis=2, concat_axis=0, tiled=True
    ).astype(summed_rows.dtype)
    bias_low = bias_tile.astype(jnp.bfloat16)
    pair_hat, pair_inv = layer_statistics(pairwise_features.astype(jnp.float32))
    pair_normed_grad = jnp.einsum(
        "hij,ch->ijc", bias_low, pairwise_weight, preferred_element_type=jnp.float32
    )
    pairwise_gradient = layer_reverse_step(
        pair_normed_grad * pairwise_norm_gain, pair_hat, pair_inv
    ).astype(jnp.bfloat16)
    return (alignment_input_gradient, pairwise_gradient)


def solution(mesh):
    placed = (
        P("seq", None, None),
        P(None, "seq", None),
        P("head", "seq", None),
        P("seq", "head", None),
        P(),
        P(),
        P(),
        P(),
        P(),
        P(),
        P(),
        P(),
        P(),
        P(),
    )
    return jax.shard_map(
        per_device,
        mesh=mesh,
        in_specs=placed,
        out_specs=(P("seq", "head", None), P("seq", "head", None)),
        check_vma=False,
    )
```

profile of v0, /device:TPU:10, one launch (start us, length us, event | category | flops | bytes accessed | tf_op | source)
XLA Modules:
  0.0 1444.2 jit_solution(13815604666751804673)
XLA Ops:
  66.9 91.8 %all-to-all-done = bf16[128,64,256]{2,1,0:T(8,128)(2,1)} async-done(((bf16[128,64,256]{2,1,0:T(8,128)(2,1)}), bf16[128,64,256]{2,1,0:T(8,128)(2,1)}, u32[]{:S(2)}, u32[]{:S(2)}) %all-to-all-start) | async-done | bytes 4194336 | tf_op jit(solution)/shard_map/all_to_all | solution.py:67
  164.1 15.8 %copy.64 = f32[4,1024,1024]{1,2,0:T(8,128)} copy(bf16[4,1024,1024]{2,0,1:T(4,128)(2,1)} %all-gather.2.cloned.1.call-done) | data formatting | bytes 25165824
  179.9 810.9 %while.13 = (s32[]{:T(128)}, f32[4,1024,1024]{1,2,0:T(8,128)}, bf16[8,1024,4,128]{1,3,2,0:T(8,128)(2,1)}, bf16[8,1024,4,32]{1,3,2,0:T(8,128)(2,1)}, bf16[8,1024,...) while((s32[]{:T(128)}, f32[4,1024,1024]{1,2,0:T(8,128)}, ...), condition=%wide.region_6.7_spmd.clone, body=%wide.region_2.6_spmd.clone.sunk | while | flops 1692408832 | bytes 267244176 | solution.py:109
  180.2 13.9 convolution_add_fusion.2
  194.1 18.6 %fusion.127 = (f32[4,1024]{1,0:T(4,128)S(1)}, f32[4,1024,1024]{1,2,0:T(8,128)}) fusion(f32[4,1024,1024]{1,2,0:T(8,128)} %convolution_add_fusion.2), kind=kOutput, calls=%fused_computation.106.clone.1 | output fusion | flops 8389631 | bytes 33570816 | tf_op jit(solution)/shard_map/while/body/eval_jaxpr/sub | solution.py:82
  212.7 14.3 multiply_reduce_fusion.4
  227.0 17.3 %fusion.128 = (bf16[4,1024,1024]{1,2,0:T(8,128)(2,1)S(1)}, f32[4,1024,1024]{1,2,0:T(8,128)}) fusion(f32[4,1024,1024]{1,2,0:T(8,128)} %get-tuple-element.193, f32[4,1024]{1,0:T(4,128)S(1)} %get-tuple-element.194, f32[4,1024,1024]{1,2,0:T(8,128)} %get-tuple-element.191, f32[4,1024]{1,0:T(4,128)S(1)} %get-tuple-element.192, ...), kind=kLoop, calls=%fused_computation.7.clone.1 | loop fusion | flops 25165824 | bytes 75530240 | tf_op jit(solution)/shard_map/while/body/eval_jaxpr/convert_element_type | solution.py:95
  290.2 18.6 %fusion.127 = (f32[4,1024]{1,0:T(4,128)S(1)}, f32[4,1024,1024]{1,2,0:T(8,128)}) fusion(f32[4,1024,1024]{1,2,0:T(8,128)} %convolution_add_fusion.2), kind=kOutput, calls=%fused_computation.106.clone.1 | output fusion | flops 8389631 | bytes 33570816 | tf_op jit(solution)/shard_map/while/body/eval_jaxpr/sub | solution.py:82
  308.8 14.3 multiply_reduce_fusion.4
  323.1 23.3 %fusion.128 = (bf16[4,1024,1024]{1,2,0:T(8,128)(2,1)S(1)}, f32[4,1024,1024]{1,2,0:T(8,128)}) fusion(f32[4,1024,1024]{1,2,0:T(8,128)} %get-tuple-element.193, f32[4,1024]{1,0:T(4,128)S(1)} %get-tuple-element.194, f32[4,1024,1024]{1,2,0:T(8,128)} %get-tuple-element.191, f32[4,1024]{1,0:T(4,128)S(1)} %get-tuple-element.192, ...), kind=kLoop, calls=%fused_computation.7.clone.1 | loop fusion | flops 25165824 | bytes 75530240 | tf_op jit(solution)/shard_map/while/body/eval_jaxpr/convert_element_type | solution.py:95
  392.2 18.6 %fusion.127 = (f32[4,1024]{1,0:T(4,128)S(1)}, f32[4,1024,1024]{1,2,0:T(8,128)}) fusion(f32[4,1024,1024]{1,2,0:T(8,128)} %convolution_add_fusion.2), kind=kOutput, calls=%fused_computation.106.clone.1 | output fusion | flops 8389631 | bytes 33570816 | tf_op jit(solution)/shard_map/while/body/eval_jaxpr/sub | solution.py:82
  410.8 14.3 multiply_reduce_fusion.4
  425.1 23.3 %fusion.128 = (bf16[4,1024,1024]{1,2,0:T(8,128)(2,1)S(1)}, f32[4,1024,1024]{1,2,0:T(8,128)}) fusion(f32[4,1024,1024]{1,2,0:T(8,128)} %get-tuple-element.193, f32[4,1024]{1,0:T(4,128)S(1)} %get-tuple-element.194, f32[4,1024,1024]{1,2,0:T(8,128)} %get-tuple-element.191, f32[4,1024]{1,0:T(4,128)S(1)} %get-tuple-element.192, ...), kind=kLoop, calls=%fused_computation.7.clone.1 | loop fusion | flops 25165824 | bytes 75530240 | tf_op jit(solution)/shard_map/while/body/eval_jaxpr/convert_element_type | solution.py:95
  494.3 18.6 %fusion.127 = (f32[4,1024]{1,0:T(4,128)S(1)}, f32[4,1024,1024]{1,2,0:T(8,128)}) fusion(f32[4,1024,1024]{1,2,0:T(8,128)} %convolution_add_fusion.2), kind=kOutput, calls=%fused_computation.106.clone.1 | output fusion | flops 8389631 | bytes 33570816 | tf_op jit(solution)/shard_map/while/body/eval_jaxpr/sub | solution.py:82
  512.9 14.3 multiply_reduce_fusion.4
  527.2 23.3 %fusion.128 = (bf16[4,1024,1024]{1,2,0:T(8,128)(2,1)S(1)}, f32[4,1024,1024]{1,2,0:T(8,128)}) fusion(f32[4,1024,1024]{1,2,0:T(8,128)} %get-tuple-element.193, f32[4,1024]{1,0:T(4,128)S(1)} %get-tuple-element.194, f32[4,1024,1024]{1,2,0:T(8,128)} %get-tuple-element.191, f32[4,1024]{1,0:T(4,128)S(1)} %get-tuple-element.192, ...), kind=kLoop, calls=%fused_computation.7.clone.1 | loop fusion | flops 25165824 | bytes 75530240 | tf_op jit(solution)/shard_map/while/body/eval_jaxpr/convert_element_type | solution.py:95
  582.4 13.9 convolution_add_fusion.2
  596.4 18.6 %fusion.127 = (f32[4,1024]{1,0:T(4,128)S(1)}, f32[4,1024,1024]{1,2,0:T(8,128)}) fusion(f32[4,1024,1024]{1,2,0:T(8,128)} %convolution_add_fusion.2), kind=kOutput, calls=%fused_computation.106.clone.1 | output fusion | flops 8389631 | bytes 33570816 | tf_op jit(solution)/shard_map/while/body/eval_jaxpr/sub | solution.py:82
  615.0 14.3 multiply_reduce_fusion.4
  629.3 23.3 %fusion.128 = (bf16[4,1024,1024]{1,2,0:T(8,128)(2,1)S(1)}, f32[4,1024,1024]{1,2,0:T(8,128)}) fusion(f32[4,1024,1024]{1,2,0:T(8,128)} %get-tuple-element.193, f32[4,1024]{1,0:T(4,128)S(1)} %get-tuple-element.194, f32[4,1024,1024]{1,2,0:T(8,128)} %get-tuple-element.191, f32[4,1024]{1,0:T(4,128)S(1)} %get-tuple-element.192, ...), kind=kLoop, calls=%fused_computation.7.clone.1 | loop fusion | flops 25165824 | bytes 75530240 | tf_op jit(solution)/shard_map/while/body/eval_jaxpr/convert_element_type | solution.py:95
  698.4 18.6 %fusion.127 = (f32[4,1024]{1,0:T(4,128)S(1)}, f32[4,1024,1024]{1,2,0:T(8,128)}) fusion(f32[4,1024,1024]{1,2,0:T(8,128)} %convolution_add_fusion.2), kind=kOutput, calls=%fused_computation.106.clone.1 | output fusion | flops 8389631 | bytes 33570816 | tf_op jit(solution)/shard_map/while/body/eval_jaxpr/sub | solution.py:82
  717.0 14.3 multiply_reduce_fusion.4
  731.3 23.3 %fusion.128 = (bf16[4,1024,1024]{1,2,0:T(8,128)(2,1)S(1)}, f32[4,1024,1024]{1,2,0:T(8,128)}) fusion(f32[4,1024,1024]{1,2,0:T(8,128)} %get-tuple-element.193, f32[4,1024]{1,0:T(4,128)S(1)} %get-tuple-element.194, f32[4,1024,1024]{1,2,0:T(8,128)} %get-tuple-element.191, f32[4,1024]{1,0:T(4,128)S(1)} %get-tuple-element.192, ...), kind=kLoop, calls=%fused_computation.7.clone.1 | loop fusion | flops 25165824 | bytes 75530240 | tf_op jit(solution)/shard_map/while/body/eval_jaxpr/convert_element_type | solution.py:95
  786.5 13.9 convolution_add_fusion.2
  800.5 18.6 %fusion.127 = (f32[4,1024]{1,0:T(4,128)S(1)}, f32[4,1024,1024]{1,2,0:T(8,128)}) fusion(f32[4,1024,1024]{1,2,0:T(8,128)} %convolution_add_fusion.2), kind=kOutput, calls=%fused_computation.106.clone.1 | output fusion | flops 8389631 | bytes 33570816 | tf_op jit(solution)/shard_map/while/body/eval_jaxpr/sub | solution.py:82
  819.1 14.3 multiply_reduce_fusion.4
  833.4 23.3 %fusion.128 = (bf16[4,1024,1024]{1,2,0:T(8,128)(2,1)S(1)}, f32[4,1024,1024]{1,2,0:T(8,128)}) fusion(f32[4,1024,1024]{1,2,0:T(8,128)} %get-tuple-element.193, f32[4,1024]{1,0:T(4,128)S(1)} %get-tuple-element.194, f32[4,1024,1024]{1,2,0:T(8,128)} %get-tuple-element.191, f32[4,1024]{1,0:T(4,128)S(1)} %get-tuple-element.192, ...), kind=kLoop, calls=%fused_computation.7.clone.1 | loop fusion | flops 25165824 | bytes 75530240 | tf_op jit(solution)/shard_map/while/body/eval_jaxpr/convert_element_type | solution.py:95
  902.5 18.6 %fusion.127 = (f32[4,1024]{1,0:T(4,128)S(1)}, f32[4,1024,1024]{1,2,0:T(8,128)}) fusion(f32[4,1024,1024]{1,2,0:T(8,128)} %convolution_add_fusion.2), kind=kOutput, calls=%fused_computation.106.clone.1 | output fusion | flops 8389631 | bytes 33570816 | tf_op jit(solution)/shard_map/while/body/eval_jaxpr/sub | solution.py:82
  921.1 14.3 multiply_reduce_fusion.4
  935.4 23.3 %fusion.128 = (bf16[4,1024,1024]{1,2,0:T(8,128)(2,1)S(1)}, f32[4,1024,1024]{1,2,0:T(8,128)}) fusion(f32[4,1024,1024]{1,2,0:T(8,128)} %get-tuple-element.193, f32[4,1024]{1,0:T(4,128)S(1)} %get-tuple-element.194, f32[4,1024,1024]{1,2,0:T(8,128)} %get-tuple-element.191, f32[4,1024]{1,0:T(4,128)S(1)} %get-tuple-element.192, ...), kind=kLoop, calls=%fused_computation.7.clone.1 | loop fusion | flops 25165824 | bytes 75530240 | tf_op jit(solution)/shard_map/while/body/eval_jaxpr/convert_element_type | solution.py:95
  990.8 20.2 %copy.73 = f32[4,1024,1024]{2,0,1:T(4,128)} copy(f32[4,1024,1024]{1,2,0:T(8,128)} %get-tuple-element.51) | data formatting | bytes 33554432 | tf_op jit(solution)/shard_map/while | solution.py:109
  1018.8 364.2 %all-reduce.2 = bf16[4,1024,1024]{2,0,1:T(4,128)(2,1)} all-reduce(f32[4,1024,1024]{2,0,1:T(4,128)} %copy.73), channel_id=3, replica_groups=mesh['seq'=16,'head'=2] {'seq'}, use_global_device_ids=true, to_apply=%region_12.13.clone | all-reduce | flops 4194304 | bytes 25165824
  (138 shorter events, 450.7 us)
Async XLA Ops:
  7.2 154.0 %copy-start = (bf16[256,256]{1,0:T(8,128)(2,1)S(1)}, bf16[256,256]{1,0:T(8,128)(2,1)}, u32[]{:S(2)}) copy-start(bf16[256,256]{1,0:T(8,128)(2,1)} %param.27) | copy-start | bytes 393220
  7.2 8.8 copy-start.10
  7.2 8.9 copy-start.11
  7.2 9.0 copy-start.12
  7.2 9.1 copy-start.13
  7.2 156.8 %all-gather.2.cloned.1.call-start = ((), (), s32[]{:S(2)}) async-start(), calls=%async_computation.3 | async-start | bytes 8912896 | tf_op jit(solution)/shard_map/all_gather | solution.py:48
  9.7 149.0 %all-to-all-start = ((bf16[128,64,256]{2,1,0:T(8,128)(2,1)}), bf16[128,64,256]{2,1,0:T(8,128)(2,1)}, u32[]{:S(2)}, u32[]{:S(2)}) async-start(bf16[128,64,256]{2,1,0:T(8,128)(2,1)} %param.17), calls=%async_computation | async-start | bytes 8388608 | tf_op jit(solution)/shard_map/all_to_all | solution.py:67
  15.9 1411.7 %reduce-scatter.2.cloned.1.call-start = ((), (), s32[]{:S(2)}) async-start(), calls=%async_computation.4 | async-start | bytes 6291456 | tf_op jit(solution)/shard_map/reduce_scatter | solution.py:131
  16.5 12.9 copy-start.18
  16.5 13.0 copy-start.20
  30.7 8.4 copy-start.2
  30.7 10.5 copy-start.3
  30.7 10.5 copy-start.14
  30.7 10.5 copy-start.19
  39.1 22.8 %copy-start.8 = (f32[8,1024]{1,0:T(8,128)}, f32[8,1024]{1,0:T(8,128)S(1)}, u32[]{:S(2)}) copy-start(f32[8,1024]{1,0:T(8,128)S(1)} %add_rsqrt_fusion.1) | copy-start | bytes 98308
  41.2 16.8 %copy-start.4 = (f32[64,512]{1,0:T(8,128)}, f32[64,512]{1,0:T(8,128)S(1)}, u32[]{:S(2)}) copy-start(f32[64,512]{1,0:T(8,128)S(1)} %broadcast_multiply_fusion.2) | copy-start | bytes 393220
  990.8 20.2 %copy-start.7 = (bf16[256,8,4,32]{0,3,2,1:T(8,128)(2,1)S(1)}, bf16[256,8,4,32]{0,3,2,1:T(8,128)(2,1)}, u32[]{:S(2)}) copy-start(bf16[256,8,4,32]{0,3,2,1:T(8,128)(2,1)} %copy.69) | copy-start | bytes 1572868
  1018.8 371.4 %copy-start.9 = (f32[8,1024]{1,0:T(8,128)S(1)}, f32[8,1024]{1,0:T(8,128)}, u32[]{:S(2)}) copy-start(f32[8,1024]{1,0:T(8,128)} %copy-done.8) | copy-start | bytes 98308
  1018.8 371.4 %copy-start.6 = (f32[64,512]{1,0:T(8,128)S(1)}, f32[64,512]{1,0:T(8,128)}, u32[]{:S(2)}) copy-start(f32[64,512]{1,0:T(8,128)} %fusion.60) | copy-start | bytes 393220
  1383.0 15.4 %copy-start.5 = (f32[64,512]{1,0:T(8,128)S(1)}, f32[64,512]{1,0:T(8,128)}, u32[]{:S(2)}) copy-start(f32[64,512]{1,0:T(8,128)} %copy-done.4) | copy-start | bytes 393220
  1383.0 15.4 %copy-start.16 = (f32[128]{0:T(128)S(1)}, f32[128]{0:T(128)}, u32[]{:S(2)}) copy-start(f32[128]{0:T(128)} %param.28) | copy-start | bytes 1540
  1383.0 15.4 %copy-start.17 = (bf16[128,8]{0,1:T(8,128)(2,1)S(1)}, bf16[128,8]{0,1:T(8,128)(2,1)}, u32[]{:S(2)}) copy-start(bf16[128,8]{0,1:T(8,128)(2,1)} %param.29) | copy-start | bytes 6148
  1386.6 10.1 all-to-all-start.1
  1415.6 12.0 copy-start.15
  1415.6 21.5 %copy-start.1 = (bf16[256,256]{1,0:T(8,128)(2,1)S(1)}, bf16[256,256]{1,0:T(8,128)(2,1)}, u32[]{:S(2)}) copy-start(bf16[256,256]{1,0:T(8,128)(2,1)} %param.27) | copy-start | bytes 393220
Sparse Core Ops, SparseCore 0:
  10.2 136.0 all-gather.1
  1018.9 54.2 reduce-scatter.1
where the time goes:
time: 1460 us; the launch traced here: 1440 us
  matrix products  507 us (35%)
  other arithmetic  376 us (26%)
  blocking collectives  364 us (25%)
  waiting for transfers between devices  98.3 us (7%)
  local copies, waits for them, and re-layouts  72.1 us (5%)
  between operations  15.4 us (1%)
    unnamed x1, blocking collectives  364 us
    convert_element_type x8, other arithmetic, row_reverse_step(): score_low = score_grad.astype(jnp.bfloat16)  180 us
    sub x8, other arithmetic, row_reverse_step(): probs = jax.nn.softmax(logits, axis=-1)  149 us
    dot_general x8, matrix products, row_reverse_step(): jnp.einsum('ihd,jhd->hij', attended_grad, vals_row, preferred_element_typ...  114 us
    dot_general x8, matrix products, row_reverse_step(): jnp.einsum('ihd,jhd->hij', query_row, keys_row, preferred_element_type=jn...  112 us
    dot_general x8, matrix products, row_reverse_step(): jnp.einsum('hij,ihd->jhd', probs_low, attended_grad, preferred_element_ty...  104 us
    dot_general x8, matrix products, row_reverse_step(): jnp.einsum('hij,jhd->ihd', probs_low, vals_row, preferred_element_type=jn...  103 us
    all_to_all x1, waiting for transfers between devices, per_device(): lax.all_to_all(upstream_derivative_tensor, 'seq', split_axis=0, concat_ax...  91.8 us
  transfers between devices with their start and end apart: 4, of which 2 were waited for; matrix products, arithmetic and copies ran while one was open for 6% of the time, Pallas kernels for 0%

commit v1 on v0

v1 whole, which is shorter than its diff:
```python
import jax
import jax.numpy as jnp
from jax import lax
from jax.experimental import pallas as pl
from jax.experimental.pallas import tpu as pltpu
from jax.sharding import PartitionSpec as P

SUBSPACE_WIDTH = 32


epsilon = 1e-05


def layer_statistics(values):
    average = jnp.mean(values, axis=-1, keepdims=True)
    centred = values - average
    inverse_deviation = lax.rsqrt(jnp.mean(centred * centred, axis=-1, keepdims=True) + epsilon)
    return (centred * inverse_deviation, inverse_deviation)


def layer_reverse_step(upstream, standardized_values, inverse_deviation):
    first_mean = jnp.mean(upstream, axis=-1, keepdims=True)
    second_mean = jnp.mean(upstream * standardized_values, axis=-1, keepdims=True)
    return inverse_deviation * (upstream - first_mean - standardized_values * second_mean)


def dot(left, right, left_dim, right_dim):
    return lax.dot_general(
        left, right, (((left_dim,), (right_dim,)), ((), ())), preferred_element_type=jnp.float32
    )


def attention_kernel(tile, q_ref, k_ref, v_ref, gate_ref, gd_ref, bias_ref, grads_ref, sum_ref, acc_ref):
    score_scale = SUBSPACE_WIDTH ** (-0.5)
    residues = acc_ref.shape[0]

    @pl.when(pl.program_id(0) == 0)
    def _():
        acc_ref[...] = jnp.zeros_like(acc_ref)

    keys_t = k_ref[...]
    vals_t = v_ref[...]
    key_grad = jnp.zeros((SUBSPACE_WIDTH, residues), jnp.float32)
    value_grad = jnp.zeros((SUBSPACE_WIDTH, residues), jnp.float32)
    for start in range(0, residues, tile):
        rows = slice(start, start + tile)
        query_t = q_ref[:, rows]
        query = query_t.astype(jnp.float32).T.astype(jnp.bfloat16)
        logits = dot(query, keys_t, 1, 0) + bias_ref[rows, :].astype(jnp.float32)
        top = jnp.max(logits, axis=-1, keepdims=True)
        weights = jnp.exp(logits - top)
        share = 1.0 / jnp.sum(weights, axis=-1, keepdims=True)
        weights_low = weights.astype(jnp.bfloat16)
        attended = dot(weights_low, vals_t, 1, 1) * share
        gate_t = gate_ref[:, rows]
        grad_t = gd_ref[:, rows].astype(jnp.float32)
        out_grad = (grad_t * gate_t).astype(jnp.bfloat16).astype(jnp.float32).T
        scaled = out_grad * share
        inner = jnp.sum(scaled * attended, axis=-1, keepdims=True)
        prob_grad = dot(scaled.astype(jnp.bfloat16), vals_t, 1, 0)
        score_grad = weights * (prob_grad - inner)
        acc_ref[rows, :] += score_grad
        score_low = score_grad.astype(jnp.bfloat16)
        query_grad = score_scale * dot(score_low, keys_t, 1, 1)
        key_grad += dot(query_t, score_low, 1, 0)
        value_grad += dot(scaled.T.astype(jnp.bfloat16), weights_low, 1, 0)
        gate_grad = grad_t * attended.T * gate_t * (1.0 - gate_t)
        grads_ref[0, :, rows] = query_grad.T.astype(jnp.bfloat16)
        grads_ref[3, :, rows] = gate_grad.astype(jnp.bfloat16)
    grads_ref[1] = key_grad.astype(jnp.bfloat16)
    grads_ref[2] = value_grad.astype(jnp.bfloat16)

    @pl.when(pl.program_id(0) == pl.num_programs(0) - 1)
    def _():
        sum_ref[...] = acc_ref[...].astype(jnp.bfloat16)


def attention_reverse(head, projected, gate, gated_grad, bias_head):
    rows, _, _, width, residues = projected.shape
    tile = 256

    def part(which):
        return pl.BlockSpec(
            (None, None, None, width, residues), lambda s: (s, which, head, 0, 0)
        )

    plain = pl.BlockSpec((None, None, width, residues), lambda s: (s, head, 0, 0))
    square = rows * residues * residues
    return pl.pallas_call(
        lambda *refs: attention_kernel(tile, *refs),
        grid=(rows,),
        in_specs=[
            part(0),
            part(1),
            part(2),
            plain,
            plain,
            pl.BlockSpec((residues, residues), lambda s: (0, 0)),
        ],
        out_specs=[
            pl.BlockSpec((None, 4, width, residues), lambda s: (s, 0, 0, 0)),
            pl.BlockSpec((residues, residues), lambda s: (0, 0)),
        ],
        out_shape=[
            jax.ShapeDtypeStruct((rows, 4, width, residues), jnp.bfloat16),
            jax.ShapeDtypeStruct((residues, residues), jnp.bfloat16),
        ],
        scratch_shapes=[pltpu.VMEM((residues, residues), jnp.float32)],
        cost_estimate=pl.CostEstimate(
            flops=100 * 2 * width * square // 8, bytes_accessed=12 << 20, transcendentals=square
        ),
        compiler_params=pltpu.CompilerParams(vmem_limit_bytes=40 << 20),
        name="attention_reverse_%d" % head,
    )(projected, projected, projected, gate, gated_grad, bias_head)


def per_device(
    alignment_rows,
    upstream_derivative_tensor,
    saved_pair_bias,
    pairwise_features,
    sequence_layernorm_scaling,
    sequence_layernorm_centre,
    asking_projection_matrix,
    matching_projection_matrix,
    content_projection_matrix,
    sigmoid_projection_matrix,
    gate_offset_bias,
    final_projection_matrix,
    pairwise_norm_gain,
    pairwise_weight,
):
    local_heads = saved_pair_bias.shape[0]
    all_heads = pairwise_weight.shape[1]
    resident_rows, residue_total, channel_count = alignment_rows.shape
    head_width = local_heads * SUBSPACE_WIDTH
    first_head = lax.axis_index("head") * local_heads
    first_col = first_head * SUBSPACE_WIDTH
    score_scale = SUBSPACE_WIDTH ** (-0.5)
    biases = [
        lax.all_gather(saved_pair_bias[head], "seq", axis=0, tiled=True)
        for head in range(local_heads)
    ]
    row_grads = lax.all_to_all(
        upstream_derivative_tensor, "seq", split_axis=0, concat_axis=1, tiled=True
    )
    standardized_values, inverse_deviation = layer_statistics(alignment_rows.astype(jnp.float32))
    normalized_rows = (
        standardized_values * sequence_layernorm_scaling + sequence_layernorm_centre
    ).astype(jnp.bfloat16)

    def local(coefficient_matrix):
        return lax.dynamic_slice_in_dim(coefficient_matrix, first_col, head_width, 1)

    stacked = jnp.concatenate(
        [
            local(asking_projection_matrix),
            local(matching_projection_matrix),
            local(content_projection_matrix),
            local(sigmoid_projection_matrix),
        ],
        axis=1,
    )
    raw = jnp.einsum("cf,src->sfr", stacked, normalized_rows, preferred_element_type=jnp.float32)
    factor = jnp.where(jnp.arange(3 * head_width) < head_width, score_scale, 1.0)
    projected = (
        (raw[:, : 3 * head_width] * factor[:, None])
        .astype(jnp.bfloat16)
        .reshape(resident_rows, 3, local_heads, SUBSPACE_WIDTH, residue_total)
    )
    gate_shift = lax.dynamic_slice_in_dim(gate_offset_bias, first_col, head_width, 0)
    channel_shape = (resident_rows, local_heads, SUBSPACE_WIDTH, residue_total)
    gate = jax.nn.sigmoid(raw[:, 3 * head_width :] + gate_shift[:, None]).reshape(channel_shape)
    out_rows = lax.dynamic_slice_in_dim(final_projection_matrix, first_col, head_width, 0)
    gated_grad = (
        jnp.einsum("wc,src->swr", out_rows, row_grads, preferred_element_type=jnp.float32)
        .astype(jnp.bfloat16)
        .reshape(channel_shape)
    )
    head_grads = []
    summed_heads = []
    for head in range(local_heads):
        grads, bias_grad = attention_reverse(head, projected, gate, gated_grad, biases[head])
        head_grads.append(grads)
        summed_heads.append(lax.psum_scatter(bias_grad, "seq", scatter_dimension=0, tiled=True))
    summed_rows = jnp.stack(summed_heads)
    head_grad_rows = jnp.stack(head_grads, axis=1).reshape(
        resident_rows, local_heads, 4 * SUBSPACE_WIDTH, residue_total
    )
    piled_arrays = jnp.stack(
        [
            coefficient_matrix.reshape(channel_count, all_heads, SUBSPACE_WIDTH)
            for coefficient_matrix in (
                asking_projection_matrix,
                matching_projection_matrix,
                content_projection_matrix,
                sigmoid_projection_matrix,
            )
        ],
        axis=2,
    )
    piled_arrays = piled_arrays.reshape(channel_count, all_heads, 4 * SUBSPACE_WIDTH)
    local_weight = lax.dynamic_slice_in_dim(piled_arrays, first_head, local_heads, 1)
    partial_term = jnp.einsum(
        "shfr,chf->src", head_grad_rows, local_weight, preferred_element_type=jnp.float32
    )
    normalized_gradient = lax.psum_scatter(
        partial_term.astype(jnp.bfloat16), "head", scatter_dimension=1, tiled=True
    ).astype(jnp.float32)
    block_len = residue_total // lax.axis_size("head")
    block_start = lax.axis_index("head") * block_len
    normalized_block = lax.dynamic_slice_in_dim(standardized_values, block_start, block_len, 1)
    inverse_spread_block = lax.dynamic_slice_in_dim(inverse_deviation, block_start, block_len, 1)
    alignment_input_gradient = layer_reverse_step(
        normalized_gradient * sequence_layernorm_scaling, normalized_block, inverse_spread_block
    ).astype(jnp.bfloat16)
    bias_tile = lax.all_to_all(
        summed_rows.astype(jnp.bfloat16), "head", split_axis=2, concat_axis=0, tiled=True
    ).astype(summed_rows.dtype)
    bias_low = bias_tile.astype(jnp.bfloat16)
    pair_hat, pair_inv = layer_statistics(pairwise_features.astype(jnp.float32))
    pair_normed_grad = jnp.einsum(
        "hij,ch->ijc", bias_low, pairwise_weight, preferred_element_type=jnp.float32
    )
    pairwise_gradient = layer_reverse_step(
        pair_normed_grad * pairwise_norm_gain, pair_hat, pair_inv
    ).astype(jnp.bfloat16)
    return (alignment_input_gradient, pairwise_gradient)


def solution(mesh):
    placed = (
        P("seq", None, None),
        P(None, "seq", None),
        P("head", "seq", None),
        P("seq", "head", None),
        P(),
        P(),
        P(),
        P(),
        P(),
        P(),
        P(),
        P(),
        P(),
        P(),
    )
    return jax.shard_map(
        per_device,
        mesh=mesh,
        in_specs=placed,
        out_specs=(P("seq", "head", None), P("seq", "head", None)),
        check_vma=False,
    )
```

time: 1460 us -> 576 us (0.39)
  the two profiles are of different devices: /device:TPU:10 before, /device:TPU:0 now
where the time goes in v1:
time: 576 us; the launch traced here: 568 us
  waiting for transfers between devices  234 us (41%)
  Pallas kernels  156 us (27%)
  local copies, waits for them, and re-layouts  79.9 us (14%)
  other arithmetic  54.6 us (9%)
  matrix products  17.6 us (3%)
  between operations  14.9 us (3%)
  starting transfers between devices  11.3 us (2%)
    pallas_call x4, Pallas kernels, attention_reverse(): pl.pallas_call(lambda *refs: attention_kernel(tile, *refs), grid=(rows,),...  156 us
    reduce_scatter x4, waiting for transfers between devices, per_device(): lax.psum_scatter(bias_grad, 'seq', scatter_dimension=0, tiled=True)  150 us
    all_to_all x1, waiting for transfers between devices, per_device(): lax.all_to_all(upstream_derivative_tensor, 'seq', split_axis=0, concat_ax...  59.7 us
    unnamed x76, local copies, waits for them, and re-layouts  58.9 us
    another operation x4, local copies, waits for them, and re-layouts, per_device(): jnp.stack(head_grads, axis=1)  14.8 us
    all_to_all x1, waiting for transfers between devices, per_device(): lax.all_to_all(summed_rows.astype(jnp.bfloat16), 'head', split_axis=2, co...  12.9 us
  transfers between devices with their start and end apart: 11, of which 6 were waited for; matrix products, arithmetic and copies ran while one was open for 19% of the time, Pallas kernels for 27%

profile of v1, /device:TPU:0, one launch (start us, length us, event | category | flops | bytes accessed | tf_op | source)
XLA Modules:
  0.0 567.5 jit_solution(14991655232751190059)
XLA Ops:
  10.1 7.4 %all-to-all-start = ((bf16[128,64,256]{2,1,0:T(8,128)(2,1)}), bf16[128,64,256]{2,1,0:T(8,128)(2,1)}, u32[]{:S(2)}, u32[]{:S(2)}) async-start(bf16[128,64,256]{2,1,0:T(8,128)(2,1)} %param.15), calls=%async_computation | async-start | bytes 8388608 | tf_op jit(solution)/shard_map/all_to_all | solution.py:144
  19.5 3.6 convert_reduce_fusion.1
  23.2 4.0 fusion.12
  27.2 2.5 convolution_bitcast_fusion
  29.8 5.7 %copy-done.19 = f32[8,512,1024]{2,1,0:T(8,128)} copy-done((f32[8,512,1024]{2,1,0:T(8,128)}, f32[8,512,1024]{2,1,0:T(8,128)S(1)}, u32[]{:S(2)}) %copy-start.19) | copy-done | bytes 16777240
  35.5 3.1 fusion.24
  38.6 9.3 %fusion.9 = bf16[8,384,1024]{2,1,0:T(8,128)(2,1)} fusion(f32[8,512,1024]{2,1,0:T(8,128)} %copy-done.19, f32[384]{0:T(512)S(1)} %fusion.45), kind=kLoop, calls=%fused_computation.13 | loop fusion | flops 6291456 | bytes 18875904 | tf_op jit(solution)/shard_map/convert_element_type | solution.py:168
  48.0 59.7 %all-to-all-done = bf16[128,64,256]{2,1,0:T(8,128)(2,1)} async-done(((bf16[128,64,256]{2,1,0:T(8,128)(2,1)}), bf16[128,64,256]{2,1,0:T(8,128)(2,1)}, u32[]{:S(2)}, u32[]{:S(2)}) %all-to-all-start) | async-done | bytes 4194336 | tf_op jit(solution)/shard_map/all_to_all | solution.py:144
  107.7 2.5 copy.54
  115.6 39.0 %attention_reverse_3.1 = (bf16[8,4,32,1024]{3,2,1,0:T(8,128)(2,1)S(1)}, bf16[1024,1024]{1,0:T(8,128)(2,1)S(1)}) custom-call(bf16[8,3,4,32,1024]{4,3,2,1,0:T(8,128)(2,1)} %bitcast.70, bf16[8,3,4,32,1024]{4,3,2,1,0:T(8,128)(2,1)} %bitcast.71, bf16[8,3,4,32,1024]{4,3,2,1,0:T(8,128)(2,1)} %bitcast.72, f32[8,4,32,1024]{3,2,1,0:T(8,128)S(1)} %bitcast.54, ...), custom_call_target="tpu_custom_call" | custom-call | flops 6710886400 | bytes 12582912 | tf_op jit(solution)/shard_map/attention_reverse_3/pallas_call | solution.py:89
  161.2 38.8 %attention_reverse_2.1 = (bf16[8,4,32,1024]{3,2,1,0:T(8,128)(2,1)S(1)}, bf16[1024,1024]{1,0:T(8,128)(2,1)S(1)}) custom-call(bf16[8,3,4,32,1024]{4,3,2,1,0:T(8,128)(2,1)} %bitcast.73, bf16[8,3,4,32,1024]{4,3,2,1,0:T(8,128)(2,1)} %bitcast.74, bf16[8,3,4,32,1024]{4,3,2,1,0:T(8,128)(2,1)} %bitcast.75, f32[8,4,32,1024]{3,2,1,0:T(8,128)S(1)} %bitcast.55, ...), custom_call_target="tpu_custom_call" | custom-call | flops 6710886400 | bytes 12582912 | tf_op jit(solution)/shard_map/attention_reverse_2/pallas_call | solution.py:89
  206.6 39.0 %attention_reverse_1.1 = (bf16[8,4,32,1024]{3,2,1,0:T(8,128)(2,1)S(1)}, bf16[1024,1024]{1,0:T(8,128)(2,1)S(1)}) custom-call(bf16[8,3,4,32,1024]{4,3,2,1,0:T(8,128)(2,1)} %bitcast.76, bf16[8,3,4,32,1024]{4,3,2,1,0:T(8,128)(2,1)} %bitcast.77, bf16[8,3,4,32,1024]{4,3,2,1,0:T(8,128)(2,1)} %bitcast.78, f32[8,4,32,1024]{3,2,1,0:T(8,128)S(1)} %bitcast.56, ...), custom_call_target="tpu_custom_call" | custom-call | flops 6710886400 | bytes 12582912 | tf_op jit(solution)/shard_map/attention_reverse_1/pallas_call | solution.py:89
  252.4 38.8 %attention_reverse_0.1 = (bf16[8,4,32,1024]{3,2,1,0:T(8,128)(2,1)S(1)}, bf16[1024,1024]{1,0:T(8,128)(2,1)S(1)}) custom-call(bf16[8,3,4,32,1024]{4,3,2,1,0:T(8,128)(2,1)} %bitcast.79, bf16[8,3,4,32,1024]{4,3,2,1,0:T(8,128)(2,1)} %bitcast.80, bf16[8,3,4,32,1024]{4,3,2,1,0:T(8,128)(2,1)} %bitcast.81, f32[8,4,32,1024]{3,2,1,0:T(8,128)S(1)} %bitcast.57, ...), custom_call_target="tpu_custom_call" | custom-call | flops 6710886400 | bytes 12582912 | tf_op jit(solution)/shard_map/attention_reverse_0/pallas_call | solution.py:89
  294.1 4.4 copy.58
  300.8 4.1 copy.56
  304.9 4.0 copy.55
  308.9 5.9 %bitcast_convert_fusion = bf16[8,1024,256]{2,1,0:T(8,128)(2,1)} fusion(bf16[8,1,128,1024]{2,3,1,0:T(8,128)(2,1)S(1)} %copy-done.22, bf16[8,1,128,1024]{2,3,1,0:T(8,128)(2,1)} %copy.57, bf16[8,1,128,1024]{2,3,1,0:T(8,128)(2,1)} %copy.56, bf16[8,1,128,1024]{2,3,1,0:T(8,128)(2,1)} %copy.55, bf16[256,8,128]{0,2,1:T(8,128)(2,1)S(1)} %bitcast.92, s32[]{:T(128)S(6)} %select_n.26), kind=kOutput, calls=%fused_computation.28 | convolution fusion | flops 2162163712 | bytes 12845060 | tf_op jit(solution)/shard_map/shfr,chf->src/dot_general | solution.py:204
  314.8 12.0 %copy.65 = bf16[64,512,128]{1,2,0:T(8,128)(2,1)} copy(bf16[64,512,128]{2,1,0:T(8,128)(2,1)} %param.17) | data formatting | bytes 16777216 | tf_op args[3]
  326.7 5.9 %convert_reduce_fusion = f32[64,512]{1,0:T(8,128)S(1)} fusion(bf16[64,512,128]{1,2,0:T(8,128)(2,1)} %copy.65), kind=kLoop, calls=%fused_computation.1 | loop fusion | flops 8355840 | bytes 8519680 | tf_op jit(solution)/shard_map/reduce_sum | solution.py:15
  332.7 5.2 fusion.10
  337.9 3.1 fusion.8
  341.1 21.1 %reduce-scatter.12.cloned.1.call-done = bf16[64,1024]{1,0:T(8,128)(2,1)} async-done(((bf16[1024,1024]{1,0:T(8,128)(2,1)}), bf16[64,1024]{1,0:T(8,128)(2,1)}) %reduce-scatter.12.cloned.1.call-update) | async-done | bytes 131088 | tf_op jit(solution)/shard_map/reduce_scatter | solution.py:185
  362.2 64.5 %reduce-scatter.10.cloned.1.call-done = bf16[64,1024]{1,0:T(8,128)(2,1)} async-done(((bf16[1024,1024]{1,0:T(8,128)(2,1)}), bf16[64,1024]{1,0:T(8,128)(2,1)}) %reduce-scatter.10.cloned.1.call-update) | async-done | bytes 131088 | tf_op jit(solution)/shard_map/reduce_scatter | solution.py:185
  426.7 64.5 %reduce-scatter.8.cloned.1.call-done = bf16[64,1024]{1,0:T(8,128)(2,1)} async-done(((bf16[1024,1024]{1,0:T(8,128)(2,1)}), bf16[64,1024]{1,0:T(8,128)(2,1)}) %reduce-scatter.8.cloned.1.call-update) | async-done | bytes 131088 | tf_op jit(solution)/shard_map/reduce_scatter | solution.py:185
  494.7 3.5 all-to-all-start.1
  498.2 12.9 %all-to-all-done.1 = bf16[2,2,65536]{2,1,0:T(2,128)(2,1)S(1)} async-done(((bf16[2,2,65536]{2,1,0:T(2,128)(2,1)}), bf16[2,2,65536]{2,1,0:T(2,128)(2,1)S(1)}, u32[]{:S(2)}, u32[]{:S(2)}) %all-to-all-start.1) | async-done | bytes 524320 | tf_op jit(solution)/shard_map/all_to_all | solution.py:217
  513.0 7.7 %multiply_reduce_fusion = (f32[64,512]{1,0:T(8,128)S(1)}, f32[64,512]{1,0:T(8,128)S(1)}, f32[64,512,128]{1,2,0:T(8,128)S(1)}) fusion(f32[128]{0:T(128)S(1)} %copy-done.29, f32[64,512]{1,0:T(8,128)S(1)} %add_rsqrt_fusion, f32[64,512]{1,0:T(8,128)S(1)} %broadcast_multiply_fusion.2, bf16[64,512,128]{1,2,0:T(8,128)(2,1)} %copy.65, ...), kind=kOutput, calls=%fused_computation.11 | convolution fusion | flops 96403456 | bytes 26216960 | tf_op jit(solution)/shard_map/hij,ch->ijc/dot_general | solution.py:222
  520.8 9.5 %fusion.7 = bf16[64,512,128]{1,2,0:T(8,128)(2,1)} fusion(bf16[64,512,128]{1,2,0:T(8,128)(2,1)} %copy.65, f32[64,512,128]{1,2,0:T(8,128)S(1)} %get-tuple-element.32, f32[64,512]{1,0:T(8,128)S(1)} %broadcast_multiply_fusion, f32[64,512]{1,0:T(8,128)S(1)} %broadcast_multiply_fusion.1, f32[128]{0:T(128)S(1)} %copy-done.29, f32[64,512]{1,0:T(8,128)S(1)} %add_rsqrt_fusion, ...), kind=kLoop, calls=%fused_computation.9 | loop fusion | flops 37748736 | bytes 34079232 | tf_op jit(solution)/shard_map/convert_element_type | solution.py:227
  530.3 11.9 %copy.68 = bf16[64,512,128]{2,1,0:T(8,128)(2,1)} copy(bf16[64,512,128]{1,2,0:T(8,128)(2,1)} %fusion.7) | data formatting | bytes 16777216
  542.2 8.7 %reduce-scatter.6.cloned.1.call-done = bf16[8,512,256]{2,1,0:T(8,128)(2,1)} async-done(((bf16[8,1024,256]{2,1,0:T(8,128)(2,1)}), bf16[8,512,256]{2,1,0:T(8,128)(2,1)}) %reduce-scatter.6.cloned.1.call-update) | async-done | bytes 2097168 | tf_op jit(solution)/shard_map/reduce_scatter | solution.py:207
  551.0 4.0 fusion.25
  555.0 5.5 multiply_convert_fusion
  (119 shorter events, 40.7 us)
Async XLA Ops:
  7.2 103.1 %copy-start = (bf16[256,256]{1,0:T(8,128)(2,1)S(1)}, bf16[256,256]{1,0:T(8,128)(2,1)}, u32[]{:S(2)}) copy-start(bf16[256,256]{1,0:T(8,128)(2,1)} %param.25) | copy-start | bytes 393220
  7.2 11.8 %copy-start.23 = (bf16[256,256]{1,0:T(8,128)(2,1)S(1)}, bf16[256,256]{1,0:T(8,128)(2,1)}, u32[]{:S(2)}) copy-start(bf16[256,256]{1,0:T(8,128)(2,1)} %param.23) | copy-start | bytes 393220
  7.2 11.9 %copy-start.24 = (bf16[256,256]{1,0:T(8,128)(2,1)S(1)}, bf16[256,256]{1,0:T(8,128)(2,1)}, u32[]{:S(2)}) copy-start(bf16[256,256]{1,0:T(8,128)(2,1)} %param.22) | copy-start | bytes 393220
  7.2 12.0 %copy-start.25 = (bf16[256,256]{1,0:T(8,128)(2,1)S(1)}, bf16[256,256]{1,0:T(8,128)(2,1)}, u32[]{:S(2)}) copy-start(bf16[256,256]{1,0:T(8,128)(2,1)} %param.21) | copy-start | bytes 393220
  7.2 12.1 %copy-start.26 = (bf16[256,256]{1,0:T(8,128)(2,1)S(1)}, bf16[256,256]{1,0:T(8,128)(2,1)}, u32[]{:S(2)}) copy-start(bf16[256,256]{1,0:T(8,128)(2,1)} %param.20) | copy-start | bytes 393220
  7.2 12.2 %copy-start.31 = (f32[256]{0:T(256)S(1)}, f32[256]{0:T(256)}, u32[]{:S(2)}) copy-start(f32[256]{0:T(256)} %param.24) | copy-start | bytes 3076
  7.2 104.5 %all-gather.15.cloned.1.call-start = ((), (), s32[]{:S(2)}) async-start(), calls=%async_computation.15 | async-start | bytes 2228224 | tf_op jit(solution)/shard_map/all_gather | solution.py:141
  9.3 148.0 %all-gather.13.cloned.1.call-start = ((), (), s32[]{:S(2)}) async-start(), calls=%async_computation.14 | async-start | bytes 2228224 | tf_op jit(solution)/shard_map/all_gather | solution.py:141
  10.1 17.1 %copy-start.27 = (f32[256]{0:T(256)S(1)}, f32[256]{0:T(256)}, u32[]{:S(2)}) copy-start(f32[256]{0:T(256)} %param.18) | copy-start | bytes 3076
  10.1 17.1 %copy-start.28 = (f32[256]{0:T(256)S(1)}, f32[256]{0:T(256)}, u32[]{:S(2)}) copy-start(f32[256]{0:T(256)} %param.19) | copy-start | bytes 3076
  10.1 97.6 %all-to-all-start = ((bf16[128,64,256]{2,1,0:T(8,128)(2,1)}), bf16[128,64,256]{2,1,0:T(8,128)(2,1)}, u32[]{:S(2)}, u32[]{:S(2)}) async-start(bf16[128,64,256]{2,1,0:T(8,128)(2,1)} %param.15), calls=%async_computation | async-start | bytes 8388608 | tf_op jit(solution)/shard_map/all_to_all | solution.py:144
  17.6 185.3 %all-gather.11.cloned.1.call-start = ((), (), s32[]{:S(2)}) async-start(), calls=%async_computation.13 | async-start | bytes 2228224 | tf_op jit(solution)/shard_map/all_gather | solution.py:141
  18.3 230.1 %all-gather.9.cloned.1.call-start = ((), (), s32[]{:S(2)}) async-start(), calls=%async_computation.12 | async-start | bytes 2228224 | tf_op jit(solution)/shard_map/all_gather | solution.py:141
  18.9 322.2 %reduce-scatter.14.cloned.1.call-start = ((), (), s32[]{:S(2)}) async-start(), calls=%async_computation.11 | async-start | bytes 2228224 | tf_op jit(solution)/shard_map/reduce_scatter | solution.py:185
  19.4 7.8 %copy-start.20 = (bf16[8,1024,256]{2,1,0:T(8,128)(2,1)S(1)}, bf16[8,1024,256]{2,1,0:T(8,128)(2,1)}, u32[]{:S(2)}) copy-start(bf16[8,1024,256]{2,1,0:T(8,128)(2,1)} %param.14) | copy-start | bytes 12582916
  29.8 5.8 %copy-start.19 = (f32[8,512,1024]{2,1,0:T(8,128)}, f32[8,512,1024]{2,1,0:T(8,128)S(1)}, u32[]{:S(2)}) copy-start(f32[8,512,1024]{2,1,0:T(8,128)S(1)} %convolution_bitcast_fusion) | copy-start | bytes 50331652
  111.7 2.3 copy-start.2
  157.3 204.9 %reduce-scatter.12.cloned.1.call-start = ((), (), s32[]{:S(2)}) async-start(), calls=%async_computation.10 | async-start | bytes 2228224 | tf_op jit(solution)/shard_map/reduce_scatter | solution.py:185
  157.4 2.2 copy-start.3
  202.8 223.9 %reduce-scatter.10.cloned.1.call-start = ((), (), s32[]{:S(2)}) async-start(), calls=%async_computation.9 | async-start | bytes 2228224 | tf_op jit(solution)/shard_map/reduce_scatter | solution.py:185
  248.4 242.8 %reduce-scatter.8.cloned.1.call-start = ((), (), s32[]{:S(2)}) async-start(), calls=%async_computation.8 | async-start | bytes 2228224 | tf_op jit(solution)/shard_map/reduce_scatter | solution.py:185
  248.5 2.3 copy-start.5
  293.9 4.6 copy-start.12
  293.9 257.1 %reduce-scatter.6.cloned.1.call-start = ((), (), s32[]{:S(2)}) async-start(), calls=%async_computation.7 | async-start | bytes 6291456 | tf_op jit(solution)/shard_map/reduce_scatter | solution.py:207
  300.8 8.1 %copy-start.22 = (bf16[8,1,128,1024]{2,3,1,0:T(8,128)(2,1)S(1)}, bf16[8,1,128,1024]{2,3,1,0:T(8,128)(2,1)}, u32[]{:S(2)}) copy-start(bf16[8,1,128,1024]{2,3,1,0:T(8,128)(2,1)} %copy.58) | copy-start | bytes 6291460
  326.7 5.9 %copy-start.21 = (bf16[8,1024,256]{2,1,0:T(8,128)(2,1)S(1)}, bf16[8,1024,256]{2,1,0:T(8,128)(2,1)}, u32[]{:S(2)}) copy-start(bf16[8,1024,256]{2,1,0:T(8,128)(2,1)} %param.14) | copy-start | bytes 12582916
  326.7 11.2 %slice-start = ((s8[8388608]{0:T(1024)(128)(4,1)}), s8[4194304]{0:T(1024)(128)(4,1)S(1)}, s32[]{:S(2)}) async-start(s8[8388608]{0:T(1024)(128)(4,1)} %bitcast.82), calls=%async_computation.16 | async-start | bytes 8388608
  332.6 5.2 slice-start.1
  337.9 175.1 %copy-start.29 = (f32[128]{0:T(128)S(1)}, f32[128]{0:T(128)}, u32[]{:S(2)}) copy-start(f32[128]{0:T(128)} %param.26) | copy-start | bytes 1540
  337.9 175.1 %copy-start.30 = (bf16[128,8]{0,1:T(8,128)(2,1)S(1)}, bf16[128,8]{0,1:T(8,128)(2,1)}, u32[]{:S(2)}) copy-start(bf16[128,8]{0,1:T(8,128)(2,1)} %param.27) | copy-start | bytes 6148
  494.7 16.4 %all-to-all-start.1 = ((bf16[2,2,65536]{2,1,0:T(2,128)(2,1)}), bf16[2,2,65536]{2,1,0:T(2,128)(2,1)S(1)}, u32[]{:S(2)}, u32[]{:S(2)}) async-start(bf16[2,2,65536]{2,1,0:T(2,128)(2,1)} %reshape.102), calls=%async_computation.6 | async-start | bytes 1048576 | tf_op jit(solution)/shard_map/all_to_all | solution.py:217
  530.3 30.2 %copy-start.1 = (bf16[256,256]{1,0:T(8,128)(2,1)S(1)}, bf16[256,256]{1,0:T(8,128)(2,1)}, u32[]{:S(2)}) copy-start(bf16[256,256]{1,0:T(8,128)(2,1)} %param.25) | copy-start | bytes 393220
  (13 other events, 19.4 us)
Sparse Core Ops, SparseCore 0:
  10.8 86.4 all-gather.14
  99.4 49.5 all-gather.12
  151.2 40.2 all-gather.10
  193.5 40.1 all-gather.8
  237.3 60.5 reduce-scatter.13
  301.5 60.6 reduce-scatter.11
  365.9 60.7 reduce-scatter.9
  430.5 60.7 reduce-scatter.7
  493.5 57.4 reduce-scatter.5

commit v2 on v1

--- a/solution.py
+++ b/solution.py
@@ -114,6 +114,60 @@
     )(projected, projected, projected, gate, gated_grad, bias_head)
 
 
+def pair_layout():
+    size = lax.axis_size("seq")
+    swap = [(index, index ^ 1) for index in range(size)]
+    groups = [list(range(minor, size, 2)) for minor in range(2)]
+    return swap, groups, lax.axis_index("seq") % 2
+
+
+def gather_bias(block):
+    swap, groups, minor = pair_layout()
+    own = lax.all_gather(block, "seq", axis_index_groups=groups, axis=0, tiled=False)
+    other = lax.ppermute(own, "seq", swap)
+    first = jnp.where(minor == 0, own, other)
+    second = jnp.where(minor == 0, other, own)
+    return jnp.stack([first, second], axis=1).reshape(-1, block.shape[1])
+
+
+def scatter_sum(bias_grad):
+    swap, groups, minor = pair_layout()
+    size = lax.axis_size("seq")
+    residues = bias_grad.shape[1]
+    blocks = bias_grad.reshape(size // 2, 2, residues // size, residues)
+    mine = lax.dynamic_index_in_dim(blocks, minor, 1, keepdims=False)
+    theirs = lax.dynamic_index_in_dim(blocks, 1 - minor, 1, keepdims=False)
+    received = lax.ppermute(theirs, "seq", swap)
+    half = (mine.astype(jnp.float32) + received.astype(jnp.float32)).astype(jnp.bfloat16)
+    return lax.psum_scatter(
+        half.reshape(-1, residues),
+        "seq",
+        axis_index_groups=groups,
+        scatter_dimension=0,
+        tiled=True,
+    )
+
+
+def project_back_kernel(weight_ref, *refs):
+    stacked = jnp.concatenate([ref[...] for ref in refs[:-1]], axis=0)
+    refs[-1][...] = dot(weight_ref[...], stacked, 1, 0).T.astype(jnp.bfloat16)
+
+
+def project_back(weight, head_grads):
+    rows, width, residues = head_grads[0].shape
+    channels = weight.shape[0]
+    return pl.pallas_call(
+        project_back_kernel,
+        grid=(rows,),
+        in_specs=[pl.BlockSpec(weight.shape, lambda s: (0, 0))]
+        + [pl.BlockSpec((None, width, residues), lambda s: (s, 0, 0))] * len(head_grads),
+        out_specs=pl.BlockSpec((None, residues, channels), lambda s: (s, 0, 0)),
+        out_shape=jax.ShapeDtypeStruct((rows, residues, channels), jnp.bfloat16),
+        compiler_params=pltpu.CompilerParams(vmem_limit_bytes=24 << 20),
+        name="project_back",
+    )(weight, *head_grads)
+
+
 def per_device(
     alignment_rows,
     upstream_derivative_tensor,
@@ -138,7 +192,7 @@
     first_col = first_head * SUBSPACE_WIDTH
     score_scale = SUBSPACE_WIDTH ** (-0.5)
     biases = [
-        lax.all_gather(saved_pair_bias[head], "seq", axis=0, tiled=True)
+        gather_bias(saved_pair_bias[head])
         for head in range(local_heads)
     ]
     row_grads = lax.all_to_all(
@@ -182,11 +236,8 @@
     for head in range(local_heads):
         grads, bias_grad = attention_reverse(head, projected, gate, gated_grad, biases[head])
         head_grads.append(grads)
-        summed_heads.append(lax.psum_scatter(bias_grad, "seq", scatter_dimension=0, tiled=True))
+        summed_heads.append(scatter_sum(bias_grad))
     summed_rows = jnp.stack(summed_heads)
-    head_grad_rows = jnp.stack(head_grads, axis=1).reshape(
-        resident_rows, local_heads, 4 * SUBSPACE_WIDTH, residue_total
-    )
     piled_arrays = jnp.stack(
         [
             coefficient_matrix.reshape(channel_count, all_heads, SUBSPACE_WIDTH)
@@ -201,8 +252,12 @@
     )
     piled_arrays = piled_arrays.reshape(channel_count, all_heads, 4 * SUBSPACE_WIDTH)
     local_weight = lax.dynamic_slice_in_dim(piled_arrays, first_head, local_heads, 1)
-    partial_term = jnp.einsum(
-        "shfr,chf->src", head_grad_rows, local_weight, preferred_element_type=jnp.float32
+    partial_term = project_back(
+        local_weight.reshape(channel_count, local_heads * 4 * SUBSPACE_WIDTH),
+        [
+            grads.reshape(resident_rows, 4 * SUBSPACE_WIDTH, residue_total)
+            for grads in head_grads
+        ],
     )
     normalized_gradient = lax.psum_scatter(
         partial_term.astype(jnp.bfloat16), "head", scatter_dimension=1, tiled=True

time: 576 us -> 582 us (1.010)
  local copies, waits for them, and re-layouts: 79.9 us -> 55.4 us
  other arithmetic: 54.6 us -> 77.1 us
    all_gather x4, waiting for transfers between devices: 0.08 us -> 99.3 us  [gather_bias(): lax.all_gather(block, 'seq', axis_index_groups=groups, axis=0, tiled=False)]
    all_to_all x1, waiting for transfers between devices: 59.7 us -> 0.01 us  [per_device(): lax.all_to_all(upstream_derivative_tensor, 'seq', split_axis=0, concat_ax...]
    reduce_scatter x4, waiting for transfers between devices: 150 us -> 109 us  [scatter_sum(): lax.psum_scatter(half.reshape(-1, residues), 'seq', axis_index_groups=gro...]
    unnamed x76 -> x88, local copies, waits for them, and re-layouts: 58.9 us -> 43.7 us
    another operation x0 -> x8, other arithmetic: none -> 13 us  [gather_bias(): return jnp.stack([first, second], axis=1).reshape(-1, block.shape[1])]
    another operation x5, local copies, waits for them, and re-layouts: 14.8 us -> 2.18 us  [the longest x4 2.17 us: gather_bias(): return jnp.stack([first, second], axis=1).reshape(-1, block.shape[1])]
    convert_element_type x0 -> x4, other arithmetic: none -> 8.1 us  [scatter_sum(): (mine.astype(jnp.float32) + received.astype(jnp.float32)).astype(jnp.bflo...]
    dot_general x1 -> x0, matrix products: 5.86 us -> none  [per_device(): jnp.einsum('shfr,chf->src', head_grad_rows, local_weight, preferred_eleme...]
  transfers between devices with their start and end apart: 11 -> 19, of which waited for: 6 -> 7; matrix products, arithmetic and copies ran while one was open for 19% -> 21% of each run, Pallas kernels for 27% -> 28%
where the time goes in v2:
time: 582 us; the launch traced here: 571 us
  waiting for transfers between devices  234 us (40%)
  Pallas kernels  160 us (27%)
  other arithmetic  77.1 us (13%)
  local copies, waits for them, and re-layouts  55.4 us (10%)
  matrix products  16.3 us (3%)
  between operations  14.9 us (3%)
  starting transfers between devices  13.7 us (2%)
    pallas_call x4, Pallas kernels, attention_reverse(): pl.pallas_call(lambda *refs: attention_kernel(tile, *refs), grid=(rows,),...  156 us
    reduce_scatter x4, waiting for transfers between devices, scatter_sum(): lax.psum_scatter(half.reshape(-1, residues), 'seq', axis_index_groups=gro...  109 us
    all_gather x4, waiting for transfers between devices, gather_bias(): lax.all_gather(block, 'seq', axis_index_groups=groups, axis=0, tiled=False)  99.3 us
    unnamed x88, local copies, waits for them, and re-layouts  43.7 us
    another operation x8, other arithmetic, gather_bias(): return jnp.stack([first, second], axis=1).reshape(-1, block.shape[1])  13 us
    all_to_all x1, waiting for transfers between devices, per_device(): lax.all_to_all(summed_rows.astype(jnp.bfloat16), 'head', split_axis=2, co...  13 us
  transfers between devices with their start and end apart: 19, of which 7 were waited for; matrix products, arithmetic and copies ran while one was open for 21% of the time, Pallas kernels for 28%

profile of v2, /device:TPU:0, one launch (start us, length us, event | category | flops | bytes accessed | tf_op | source)
XLA Modules:
  0.0 571.1 jit_solution(12670670080286013812)
XLA Ops:
  9.2 7.6 %all-to-all-start = ((bf16[128,64,256]{2,1,0:T(8,128)(2,1)}), bf16[128,64,256]{2,1,0:T(8,128)(2,1)}, u32[]{:S(2)}, u32[]{:S(2)}) async-start(bf16[128,64,256]{2,1,0:T(8,128)(2,1)} %param.15), calls=%async_computation | async-start | bytes 8388608 | tf_op jit(solution)/shard_map/all_to_all | solution.py:198
  19.6 3.6 convert_reduce_fusion.1
  23.2 2.4 fusion.12
  25.7 7.1 %convolution_bitcast_fusion = f32[8,512,1024]{2,1,0:T(8,128)} fusion(f32[256]{0:T(256)S(1)} %copy-done.34, f32[256]{0:T(256)S(1)} %copy-done.33, bf16[8,1024,256]{2,1,0:T(8,128)(2,1)S(1)} %copy-done.20, f32[8,1024]{1,0:T(8,128)S(1)} %add_rsqrt_fusion.1, f32[8,1024]{1,0:T(8,128)S(1)} %broadcast_multiply_fusion.3, ...), kind=kOutput, calls=%fused_computation.18 | convolution fusion | flops 2161115136 | bytes 21301248 | tf_op jit(solution)/shard_map/cf,src->sfr/dot_general | solution.py:218
  32.9 62.5 %all-gather.11.cloned.1.call-done = bf16[8,64,1024]{2,1,0:T(8,128)(2,1)} async-done(((bf16[1,64,1024]{2,1,0:T(8,128)(2,1)}), bf16[8,64,1024]{2,1,0:T(8,128)(2,1)}) %all-gather.11.cloned.1.call-update) | async-done | bytes 1048592 | tf_op jit(solution)/shard_map/all_gather | solution.py:126
  95.4 5.4 fusion.16
  100.8 9.4 %fusion.9 = bf16[8,384,1024]{2,1,0:T(8,128)(2,1)} fusion(f32[8,512,1024]{2,1,0:T(8,128)} %convolution_bitcast_fusion, f32[384]{0:T(512)S(1)} %fusion.36), kind=kLoop, calls=%fused_computation.13 | loop fusion | flops 6291456 | bytes 18875904 | tf_op jit(solution)/shard_map/convert_element_type | solution.py:222
  110.2 36.8 %all-gather.9.cloned.1.call-done = bf16[8,64,1024]{2,1,0:T(8,128)(2,1)} async-done(((bf16[1,64,1024]{2,1,0:T(8,128)(2,1)}), bf16[8,64,1024]{2,1,0:T(8,128)(2,1)}) %all-gather.9.cloned.1.call-update) | async-done | bytes 1048592 | tf_op jit(solution)/shard_map/all_gather | solution.py:126
  148.9 2.5 copy.79
  154.2 39.0 %attention_reverse_3.1 = (bf16[8,4,32,1024]{3,2,1,0:T(8,128)(2,1)S(1)}, bf16[1024,1024]{1,0:T(8,128)(2,1)S(1)}) custom-call(bf16[8,3,4,32,1024]{4,3,2,1,0:T(8,128)(2,1)} %bitcast.124, bf16[8,3,4,32,1024]{4,3,2,1,0:T(8,128)(2,1)} %bitcast.125, bf16[8,3,4,32,1024]{4,3,2,1,0:T(8,128)(2,1)} %bitcast.126, f32[8,4,32,1024]{3,2,1,0:T(8,128)S(1)} %bitcast.100, ...), custom_call_target="tpu_custom_call" | custom-call | flops 6710886400 | bytes 12582912 | tf_op jit(solution)/shard_map/attention_reverse_3/pallas_call | solution.py:89
  197.5 2.8 select_bitcast_fusion.3
  200.3 2.6 fusion.20
  205.5 38.8 %attention_reverse_2.1 = (bf16[8,4,32,1024]{3,2,1,0:T(8,128)(2,1)S(1)}, bf16[1024,1024]{1,0:T(8,128)(2,1)S(1)}) custom-call(bf16[8,3,4,32,1024]{4,3,2,1,0:T(8,128)(2,1)} %bitcast.127, bf16[8,3,4,32,1024]{4,3,2,1,0:T(8,128)(2,1)} %bitcast.128, bf16[8,3,4,32,1024]{4,3,2,1,0:T(8,128)(2,1)} %bitcast.129, f32[8,4,32,1024]{3,2,1,0:T(8,128)S(1)} %bitcast.101, ...), custom_call_target="tpu_custom_call" | custom-call | flops 6710886400 | bytes 12582912 | tf_op jit(solution)/shard_map/attention_reverse_2/pallas_call | solution.py:89
  248.6 2.8 select_bitcast_fusion.5
  251.4 2.7 fusion.21
  256.7 39.2 %attention_reverse_1.1 = (bf16[8,4,32,1024]{3,2,1,0:T(8,128)(2,1)S(1)}, bf16[1024,1024]{1,0:T(8,128)(2,1)S(1)}) custom-call(bf16[8,3,4,32,1024]{4,3,2,1,0:T(8,128)(2,1)} %bitcast.130, bf16[8,3,4,32,1024]{4,3,2,1,0:T(8,128)(2,1)} %bitcast.131, bf16[8,3,4,32,1024]{4,3,2,1,0:T(8,128)(2,1)} %bitcast.132, f32[8,4,32,1024]{3,2,1,0:T(8,128)S(1)} %bitcast.102, ...), custom_call_target="tpu_custom_call" | custom-call | flops 6710886400 | bytes 12582912 | tf_op jit(solution)/shard_map/attention_reverse_1/pallas_call | solution.py:89
  302.9 38.8 %attention_reverse_0.1 = (bf16[8,4,32,1024]{3,2,1,0:T(8,128)(2,1)S(1)}, bf16[1024,1024]{1,0:T(8,128)(2,1)S(1)}) custom-call(bf16[8,3,4,32,1024]{4,3,2,1,0:T(8,128)(2,1)} %bitcast.133, bf16[8,3,4,32,1024]{4,3,2,1,0:T(8,128)(2,1)} %bitcast.134, bf16[8,3,4,32,1024]{4,3,2,1,0:T(8,128)(2,1)} %bitcast.135, f32[8,4,32,1024]{3,2,1,0:T(8,128)S(1)} %bitcast.103, ...), custom_call_target="tpu_custom_call" | custom-call | flops 6710886400 | bytes 12582912 | tf_op jit(solution)/shard_map/attention_reverse_0/pallas_call | solution.py:89
  353.6 4.3 project_back.1
  360.0 11.9 %copy.84 = bf16[64,512,128]{1,2,0:T(8,128)(2,1)} copy(bf16[64,512,128]{2,1,0:T(8,128)(2,1)} %param.17) | data formatting | bytes 16777216 | tf_op args[3]
  371.9 5.6 convert_reduce_fusion
  377.6 5.3 fusion.10
  382.9 3.1 fusion.8
  386.0 42.5 %reduce-scatter.10.cloned.1.call-done = bf16[64,1024]{1,0:T(8,128)(2,1)} async-done(((bf16[512,1024]{1,0:T(8,128)(2,1)}), bf16[64,1024]{1,0:T(8,128)(2,1)}) %reduce-scatter.10.cloned.1.call-update) | async-done | bytes 131088 | tf_op jit(solution)/shard_map/reduce_scatter | solution.py:142
  428.5 66.6 %reduce-scatter.8.cloned.1.call-done = bf16[64,1024]{1,0:T(8,128)(2,1)} async-done(((bf16[512,1024]{1,0:T(8,128)(2,1)}), bf16[64,1024]{1,0:T(8,128)(2,1)}) %reduce-scatter.8.cloned.1.call-update) | async-done | bytes 131088 | tf_op jit(solution)/shard_map/reduce_scatter | solution.py:142
  498.6 3.5 all-to-all-start.1
  502.1 13.0 %all-to-all-done.1 = bf16[2,2,65536]{2,1,0:T(2,128)(2,1)S(1)} async-done(((bf16[2,2,65536]{2,1,0:T(2,128)(2,1)}), bf16[2,2,65536]{2,1,0:T(2,128)(2,1)S(1)}, u32[]{:S(2)}, u32[]{:S(2)}) %all-to-all-start.1) | async-done | bytes 524320 | tf_op jit(solution)/shard_map/all_to_all | solution.py:272
  517.9 7.7 %multiply_reduce_fusion = (f32[64,512]{1,0:T(8,128)S(1)}, f32[64,512]{1,0:T(8,128)S(1)}, f32[64,512,128]{1,2,0:T(8,128)S(1)}) fusion(f32[128]{0:T(128)S(1)} %copy-done.35, f32[64,512]{1,0:T(8,128)S(1)} %add_rsqrt_fusion, f32[64,512]{1,0:T(8,128)S(1)} %broadcast_multiply_fusion.2, bf16[64,512,128]{1,2,0:T(8,128)(2,1)} %copy.84, ...), kind=kOutput, calls=%fused_computation.11 | convolution fusion | flops 96403456 | bytes 26216960 | tf_op jit(solution)/shard_map/hij,ch->ijc/dot_general | solution.py:277
  525.6 9.6 %fusion.7 = bf16[64,512,128]{1,2,0:T(8,128)(2,1)} fusion(bf16[64,512,128]{1,2,0:T(8,128)(2,1)} %copy.84, f32[64,512,128]{1,2,0:T(8,128)S(1)} %get-tuple-element.42, f32[64,512]{1,0:T(8,128)S(1)} %broadcast_multiply_fusion, f32[64,512]{1,0:T(8,128)S(1)} %broadcast_multiply_fusion.1, f32[128]{0:T(128)S(1)} %copy-done.35, f32[64,512]{1,0:T(8,128)S(1)} %add_rsqrt_fusion, ...), kind=kLoop, calls=%fused_computation.9 | loop fusion | flops 37748736 | bytes 34079232 | tf_op jit(solution)/shard_map/convert_element_type | solution.py:282
  535.2 11.9 %copy.92 = bf16[64,512,128]{2,1,0:T(8,128)(2,1)} copy(bf16[64,512,128]{1,2,0:T(8,128)(2,1)} %fusion.7) | data formatting | bytes 16777216
  547.1 7.9 %reduce-scatter.6.cloned.1.call-done = bf16[8,512,256]{2,1,0:T(8,128)(2,1)} async-done(((bf16[8,1024,256]{2,1,0:T(8,128)(2,1)}), bf16[8,512,256]{2,1,0:T(8,128)(2,1)}) %reduce-scatter.6.cloned.1.call-update) | async-done | bytes 2097168 | tf_op jit(solution)/shard_map/reduce_scatter | solution.py:262
  555.0 4.1 fusion.17
  559.2 5.1 multiply_convert_fusion
  (166 shorter events, 50.0 us)
Async XLA Ops:
  7.2 144.2 %copy-start = (bf16[256,256]{1,0:T(8,128)(2,1)S(1)}, bf16[256,256]{1,0:T(8,128)(2,1)}, u32[]{:S(2)}) copy-start(bf16[256,256]{1,0:T(8,128)(2,1)} %param.25) | copy-start | bytes 393220
  7.2 88.2 %all-gather.11.cloned.1.call-start = ((), (), s32[]{:S(2)}) async-start(), calls=%async_computation.10 | async-start | bytes 1179648 | tf_op jit(solution)/shard_map/all_gather | solution.py:126
  9.2 9.8 %copy-start.29 = (bf16[256,256]{1,0:T(8,128)(2,1)S(1)}, bf16[256,256]{1,0:T(8,128)(2,1)}, u32[]{:S(2)}) copy-start(bf16[256,256]{1,0:T(8,128)(2,1)} %param.23) | copy-start | bytes 393220
  9.2 9.9 %copy-start.30 = (bf16[256,256]{1,0:T(8,128)(2,1)S(1)}, bf16[256,256]{1,0:T(8,128)(2,1)}, u32[]{:S(2)}) copy-start(bf16[256,256]{1,0:T(8,128)(2,1)} %param.22) | copy-start | bytes 393220
  9.2 10.0 %copy-start.31 = (bf16[256,256]{1,0:T(8,128)(2,1)S(1)}, bf16[256,256]{1,0:T(8,128)(2,1)}, u32[]{:S(2)}) copy-start(bf16[256,256]{1,0:T(8,128)(2,1)} %param.21) | copy-start | bytes 393220
  9.2 10.1 %copy-start.32 = (bf16[256,256]{1,0:T(8,128)(2,1)S(1)}, bf16[256,256]{1,0:T(8,128)(2,1)}, u32[]{:S(2)}) copy-start(bf16[256,256]{1,0:T(8,128)(2,1)} %param.20) | copy-start | bytes 393220
  9.2 10.2 %copy-start.37 = (f32[256]{0:T(256)S(1)}, f32[256]{0:T(256)}, u32[]{:S(2)}) copy-start(f32[256]{0:T(256)} %param.24) | copy-start | bytes 3076
  9.2 139.6 %all-to-all-start = ((bf16[128,64,256]{2,1,0:T(8,128)(2,1)}), bf16[128,64,256]{2,1,0:T(8,128)(2,1)}, u32[]{:S(2)}, u32[]{:S(2)}) async-start(bf16[128,64,256]{2,1,0:T(8,128)(2,1)} %param.15), calls=%async_computation | async-start | bytes 8388608 | tf_op jit(solution)/shard_map/all_to_all | solution.py:198
  16.8 130.2 %all-gather.9.cloned.1.call-start = ((), (), s32[]{:S(2)}) async-start(), calls=%async_computation.9 | async-start | bytes 1179648 | tf_op jit(solution)/shard_map/all_gather | solution.py:126
  17.6 179.9 %all-gather.7.cloned.1.call-start = ((), (), s32[]{:S(2)}) async-start(), calls=%async_computation.8 | async-start | bytes 1179648 | tf_op jit(solution)/shard_map/all_gather | solution.py:126
  18.3 230.2 %all-gather.5.cloned.1.call-start = ((), (), s32[]{:S(2)}) async-start(), calls=%async_computation.7 | async-start | bytes 1179648 | tf_op jit(solution)/shard_map/all_gather | solution.py:126
  18.9 367.1 %reduce-scatter.14.cloned.1.call-start = ((), (), s32[]{:S(2)}) async-start(), calls=%async_computation.15 | async-start | bytes 1179648 | tf_op jit(solution)/shard_map/reduce_scatter | solution.py:142
  19.2 6.5 %copy-start.25 = (bf16[256,256]{0,1:T(8,128)(2,1)}, bf16[256,256]{0,1:T(8,128)(2,1)S(1)}, u32[]{:S(2)}) copy-start(bf16[256,256]{0,1:T(8,128)(2,1)S(1)} %copy.71) | copy-start | bytes 393220
  19.3 6.4 %copy-start.27 = (bf16[256,256]{0,1:T(8,128)(2,1)}, bf16[256,256]{0,1:T(8,128)(2,1)S(1)}, u32[]{:S(2)}) copy-start(bf16[256,256]{0,1:T(8,128)(2,1)S(1)} %copy.70) | copy-start | bytes 393220
  95.4 51.7 %collective-permute-start.3 = (bf16[8,64,1024]{2,1,0:T(8,128)(2,1)}, bf16[8,64,1024]{2,1,0:T(8,128)(2,1)S(1)}, u32[]{:S(2)}, u32[]{:S(2)}) collective-permute-start(bf16[8,64,1024]{2,1,0:T(8,128)(2,1)} %all-gather.11.cloned.1.call-done), channel_id=1, source_target_pairs={{0,2},{2,0},{4,6},{6,4},{8,10},{10,8},{12,14},{14,12},{16,18},{18,... | collective-permute-start | bytes 3145736 | tf_op jit(solution)/shard_map/ppermute | solution.py:127
  100.8 46.3 %copy-start.24 = (bf16[8,64,1024]{2,1,0:T(8,128)(2,1)S(1)}, bf16[8,64,1024]{2,1,0:T(8,128)(2,1)}, u32[]{:S(2)}) copy-start(bf16[8,64,1024]{2,1,0:T(8,128)(2,1)} %all-gather.11.cloned.1.call-done) | copy-start | bytes 3145732
  147.0 50.5 %collective-permute-start.2 = (bf16[8,64,1024]{2,1,0:T(8,128)(2,1)}, bf16[8,64,1024]{2,1,0:T(8,128)(2,1)}, u32[]{:S(2)}, u32[]{:S(2)}) collective-permute-start(bf16[8,64,1024]{2,1,0:T(8,128)(2,1)} %all-gather.9.cloned.1.call-done), channel_id=1, source_target_pairs={{0,2},{2,0},{4,6},{6,4},{8,10},{10,8},{12,14},{14,12},{16,18},{18,... | collective-permute-start | bytes 3145736 | tf_op jit(solution)/shard_map/ppermute | solution.py:127
  197.0 3.3 collective-permute-start.7
  197.5 51.1 %collective-permute-start.1 = (bf16[8,64,1024]{2,1,0:T(8,128)(2,1)}, bf16[8,64,1024]{2,1,0:T(8,128)(2,1)}, u32[]{:S(2)}, u32[]{:S(2)}) collective-permute-start(bf16[8,64,1024]{2,1,0:T(8,128)(2,1)} %all-gather.7.cloned.1.call-done), channel_id=1, source_target_pairs={{0,2},{2,0},{4,6},{6,4},{8,10},{10,8},{12,14},{14,12},{16,18},{18,... | collective-permute-start | bytes 3145736 | tf_op jit(solution)/shard_map/ppermute | solution.py:127
  202.9 183.1 %reduce-scatter.12.cloned.1.call-start = ((), (), s32[]{:S(2)}) async-start(), calls=%async_computation.14 | async-start | bytes 1179648 | tf_op jit(solution)/shard_map/reduce_scatter | solution.py:142
  248.0 3.3 collective-permute-start.6
  248.5 48.0 %collective-permute-start = (bf16[8,64,1024]{2,1,0:T(8,128)(2,1)}, bf16[8,64,1024]{2,1,0:T(8,128)(2,1)}, u32[]{:S(2)}, u32[]{:S(2)}) collective-permute-start(bf16[8,64,1024]{2,1,0:T(8,128)(2,1)} %all-gather.5.cloned.1.call-done), channel_id=1, source_target_pairs={{0,2},{2,0},{4,6},{6,4},{8,10},{10,8},{12,14},{14,12},{16,18},{18,... | collective-permute-start | bytes 3145736 | tf_op jit(solution)/shard_map/ppermute | solution.py:127
  254.1 174.4 %reduce-scatter.10.cloned.1.call-start = ((), (), s32[]{:S(2)}) async-start(), calls=%async_computation.13 | async-start | bytes 1179648 | tf_op jit(solution)/shard_map/reduce_scatter | solution.py:142
  256.7 39.9 %copy-start.23 = (bf16[8,64,1024]{2,1,0:T(8,128)(2,1)S(1)}, bf16[8,64,1024]{2,1,0:T(8,128)(2,1)}, u32[]{:S(2)}) copy-start(bf16[8,64,1024]{2,1,0:T(8,128)(2,1)} %all-gather.5.cloned.1.call-done) | copy-start | bytes 3145732
  296.0 3.0 collective-permute-start.5
  300.4 194.8 %reduce-scatter.8.cloned.1.call-start = ((), (), s32[]{:S(2)}) async-start(), calls=%async_computation.12 | async-start | bytes 1179648 | tf_op jit(solution)/shard_map/reduce_scatter | solution.py:142
  343.2 2.9 collective-permute-start.4
  347.5 207.5 %reduce-scatter.6.cloned.1.call-start = ((), (), s32[]{:S(2)}) async-start(), calls=%async_computation.11 | async-start | bytes 6291456 | tf_op jit(solution)/shard_map/reduce_scatter | solution.py:262
  371.9 10.9 %slice-start = ((s8[8388608]{0:T(1024)(128)(4,1)}), s8[4194304]{0:T(1024)(128)(4,1)S(1)}, s32[]{:S(2)}) async-start(s8[8388608]{0:T(1024)(128)(4,1)} %bitcast.136), calls=%async_computation.16 | async-start | bytes 8388608
  497.0 20.9 %copy-start.35 = (f32[128]{0:T(128)S(1)}, f32[128]{0:T(128)}, u32[]{:S(2)}) copy-start(f32[128]{0:T(128)} %param.26) | copy-start | bytes 1540
  497.0 20.9 %copy-start.36 = (bf16[128,8]{0,1:T(8,128)(2,1)S(1)}, bf16[128,8]{0,1:T(8,128)(2,1)}, u32[]{:S(2)}) copy-start(bf16[128,8]{0,1:T(8,128)(2,1)} %param.27) | copy-start | bytes 6148
  498.6 16.5 %all-to-all-start.1 = ((bf16[2,2,65536]{2,1,0:T(2,128)(2,1)}), bf16[2,2,65536]{2,1,0:T(2,128)(2,1)S(1)}, u32[]{:S(2)}, u32[]{:S(2)}) async-start(bf16[2,2,65536]{2,1,0:T(2,128)(2,1)} %reshape.167), calls=%async_computation.6 | async-start | bytes 1048576 | tf_op jit(solution)/shard_map/all_to_all | solution.py:272
  (27 other events, 88.9 us)
Sparse Core Ops, SparseCore 0:
  10.7 84.6 all-gather.10
  97.5 49.4 all-gather.8
  149.2 38.9 all-gather.6
  190.2 38.9 all-gather.4
  232.4 62.9 reduce-scatter.13
  298.7 63.1 reduce-scatter.11
  365.3 63.1 reduce-scatter.9
  431.9 63.1 reduce-scatter.7
  497.4 57.5 reduce-scatter.5
